TPU v7x, 32 devices: a whole 2x2x4 slice. The times are simulated.
32 devices in a mesh: grp: 4 (over x, core), tp: 8 (over z, y).
Axes of the slice: x: 2, y: 2, z: 4, core: 2. Of those that a mesh axis runs over, the one named last changes fastest.
Arguments:
- acts: bfloat16 [512, 8192], P('grp', 'tp'), may hold values from -6 to 6
- cotangent: bfloat16 [512, 8192], P('tp', 'grp'), may hold values from -18 to 18
- weight: bfloat16 [8192, 8192], P('tp', 'grp'), may hold values from -0.0625 to 0.0625
- moment: float32 [8192, 8192], P('tp', 'grp'), may hold values from -3 to 3
- second: float32 [8192, 8192], P('tp', 'grp'), may hold values from 0.05 to 1
- roll_acts: bfloat16 [64, 8192], P('grp', 'tp'), may hold values from -6 to 6
- live: int32 [4], P('grp'), may hold values from 4 to 16, as said below
Outputs:
- moment_new: float32 [8192, 8192], P('tp', 'grp')
- second_new: float32 [8192, 8192], P('tp', 'grp')
- prefill_out: bfloat16 [64, 8192], P('grp', 'tp')
Inputs may be any that keep to these rules, and one draw needn't show every extreme that they name: live slots of each replica's 16; some replica is full in every draw.
All inputs are finite; a program needn't handle non-finite values.
Results may differ from a plain program's by a relative error of at most 0.023.
Values may be sent and summed in bfloat16 or wider, within the bound.
No kernel may reach another device: no remote copies, remote signals or barrier semaphores. Data moves between devices by JAX's collectives and lax.ppermute only.
A program may use at most 128 MiB of HBM per device.

v0:
```python
import jax
import jax.numpy as jnp
from jax import lax
from jax.sharding import PartitionSpec as P

E = 8192
D = 8192
beta_one = 0.9
beta_two = 0.95
learn_rate = 0.003
weight_decay = 0.1
adam_eps = 1e-08
step_count = 10


def add_terms(left, right):
    return lax.dot_general(
        left, right, (((0,), (0,)), ((), ())), preferred_element_type=jnp.float32
    )


def shards(acts, cotangent, weight, moment, second, roll_acts, live):
    cot_full = lax.all_gather(cotangent, "tp", axis=0, tiled=True)
    grad = add_terms(lax.all_gather(acts, "grp", axis=0, tiled=True), cot_full)
    total_sq = lax.psum(jnp.sum(grad * grad), ("grp", "tp"))
    factor = jnp.minimum(1.0, 1.0 / jnp.sqrt(total_sq / (E * D) + 1e-06))
    clipped = grad * factor
    moment_new = beta_one * moment + (1.0 - beta_one) * clipped
    second_new = beta_two * second + (1.0 - beta_two) * clipped * clipped
    m_hat = moment_new / (1.0 - beta_one**step_count)
    v_hat = second_new / (1.0 - beta_two**step_count)
    old = weight.astype(jnp.float32)
    weight_new = (
        old - learn_rate * (m_hat / (jnp.sqrt(v_hat) + adam_eps) + weight_decay * old)
    ).astype(jnp.bfloat16)
    slot_count = roll_acts.shape[0]
    partial_sum = jnp.dot(
        roll_acts,
        lax.all_gather(weight_new, "grp", axis=1, tiled=True),
        preferred_element_type=jnp.float32,
    )
    summed = lax.psum_scatter(
        partial_sum.astype(jnp.bfloat16), "tp", scatter_dimension=1, tiled=True
    ).astype(jnp.float32)
    slots = lax.broadcasted_iota(jnp.int32, (slot_count, 1), 0)
    alive = slots < live[0]
    prefill_out = jnp.where(alive, summed, jnp.float32(0.0)).astype(jnp.bfloat16)
    return (moment_new, second_new, prefill_out)


def solution(mesh):
    placed = (
        P("grp", "tp"),
        P("tp", "grp"),
        P("tp", "grp"),
        P("tp", "grp"),
        P("tp", "grp"),
        P("grp", "tp"),
        P("grp"),
    )
    return jax.shard_map(
        shards,
        mesh=mesh,
        in_specs=placed,
        out_specs=(P("tp", "grp"), P("tp", "grp"), P("grp", "tp")),
        check_vma=False,
    )
```

profile of v0, /device:TPU:0, one launch (start us, length us, event | category | flops | bytes accessed | tf_op | source)
XLA Modules:
  0.0 332.5 jit_solution(6522618732154518133)
XLA Ops:
  7.2 0.0 copy-start
  7.2 0.0 all-gather.4.cloned.1.call-start
  7.2 0.7 all-gather.4.cloned.1.call-update
  7.9 0.0 all-gather.6.cloned.1.call-start
  8.0 0.7 all-gather.6.cloned.1.call-update
  8.7 0.0 all-gather.8.cloned.1.call-start
  8.7 20.3 %all-gather.4.cloned.1.call-done = bf16[512,1024]{1,0:T(8,128)(2,1)} async-done(((bf16[128,1024]{1,0:T(8,128)(2,1)}), bf16[512,1024]{1,0:T(8,128)(2,1)}) %all-gather.4.cloned.1.call-update) | async-done | bytes 1048592 | tf_op jit(solution)/shard_map/all_gather | solution.py:24
  29.0 51.2 %all-gather.6.cloned.1.call-done = bf16[512,2048]{1,0:T(8,128)(2,1)} async-done(((bf16[64,2048]{1,0:T(8,128)(2,1)}), bf16[512,2048]{1,0:T(8,128)(2,1)}) %all-gather.6.cloned.1.call-update) | async-done | bytes 2097168 | tf_op jit(solution)/shard_map/all_gather | solution.py:23
  80.2 8.3 %multiply_reduce_fusion = (f32[]{:T(128)}, f32[1024,2048]{1,0:T(8,128)}) fusion(bf16[512,1024]{1,0:T(8,128)(2,1)} %all-gather.4.cloned.1.call-done, bf16[512,2048]{1,0:T(8,128)(2,1)} %all-gather.6.cloned.1.call-done), kind=kOutput, calls=%fused_computation.10 | convolution fusion | flops 2151677952 | bytes 11534340 | tf_op jit(solution)/shard_map/dot_general | solution.py:17
  88.6 39.4 %psum.7 = f32[]{:T(128)} all-reduce(f32[]{:T(128)} %get-tuple-element.6), channel_id=1, replica_groups=mesh['grp'=4,'tp'=8] {'grp','tp'}, use_global_device_ids=true, to_apply=%region_1.0 | all-reduce | flops 1 | bytes 8 | tf_op jit(solution)/shard_map/psum | solution.py:25
  128.6 18.3 %fusion.3 = (bf16[1024,2048]{1,0:T(8,128)(2,1)}, f32[1024,2048]{1,0:T(8,128)}, f32[1024,2048]{1,0:T(8,128)}) fusion(bf16[1024,2048]{1,0:T(8,128)(2,1)} %param.9, f32[1024,2048]{1,0:T(8,128)} %get-tuple-element.7, f32[]{:T(128)S(6)} %min.3, f32[1024,2048]{1,0:T(8,128)} %param.11, f32[1024,2048]{1,0:T(8,128)} %param.10), kind=kLoop, calls=%fused_computation.7 | loop fusion | flops 37748736 | bytes 50331652 | tf_op jit(solution)/shard_map/convert_element_type | solution.py:35
  147.0 0.0 all-gather.8.cloned.1.call-update
  147.0 0.0 reduce-scatter.2.cloned.1.call-start
  147.1 106.5 %all-gather.8.cloned.1.call-done = bf16[1024,8192]{1,0:T(8,128)(2,1)} async-done(((bf16[1024,2048]{1,0:T(8,128)(2,1)}), bf16[1024,8192]{1,0:T(8,128)(2,1)}) %all-gather.8.cloned.1.call-update) | async-done | bytes 16777232 | tf_op jit(solution)/shard_map/all_gather | solution.py:39
  253.5 0.0 copy-done
  253.5 8.8 %fusion = bf16[16,8192]{1,0:T(8,128)(2,1)} fusion(bf16[16,1024]{1,0:T(8,128)(2,1)S(1)} %copy-done, bf16[1024,8192]{1,0:T(8,128)(2,1)} %all-gather.8.cloned.1.call-done), kind=kOutput, calls=%fused_computation.4 | convolution fusion | flops 268566528 | bytes 17072128 | tf_op jit(solution)/shard_map/dot_general | solution.py:37
  262.3 0.0 reduce-scatter.2.cloned.1.call-update
  263.0 61.6 %reduce-scatter.2.cloned.1.call-done = bf16[16,1024]{1,0:T(8,128)(2,1)} async-done(((bf16[16,8192]{1,0:T(8,128)(2,1)}), bf16[16,1024]{1,0:T(8,128)(2,1)}) %reduce-scatter.2.cloned.1.call-update) | async-done | bytes 32784 | tf_op jit(solution)/shard_map/reduce_scatter | solution.py:42
  324.6 1.4 select_convert_fusion
  (1 shorter events, 0.0 us)
Async XLA Ops:
  7.2 246.4 %copy-start = (bf16[16,1024]{1,0:T(8,128)(2,1)S(1)}, bf16[16,1024]{1,0:T(8,128)(2,1)}, u32[]{:S(2)}) copy-start(bf16[16,1024]{1,0:T(8,128)(2,1)} %param.12) | copy-start | bytes 98308
  7.2 21.8 %all-gather.4.cloned.1.call-start = ((), (), s32[]{:S(2)}) async-start(), calls=%async_computation.1 | async-start | bytes 1310720 | tf_op jit(solution)/shard_map/all_gather | solution.py:24
  7.9 72.3 %all-gather.6.cloned.1.call-start = ((), (), s32[]{:S(2)}) async-start(), calls=%async_computation.2 | async-start | bytes 2359296 | tf_op jit(solution)/shard_map/all_gather | solution.py:23
  8.7 244.9 %all-gather.8.cloned.1.call-start = ((), (), s32[]{:S(2)}) async-start(), calls=%async_computation.3 | async-start | bytes 20971520 | tf_op jit(solution)/shard_map/all_gather | solution.py:39
  147.0 177.5 %reduce-scatter.2.cloned.1.call-start = ((), (), s32[]{:S(2)}) async-start(), calls=%async_computation.4 | async-start | bytes 294912 | tf_op jit(solution)/shard_map/reduce_scatter | solution.py:42
Sparse Core Ops, SparseCore 0:
  9.5 19.4 all-gather.3
  31.1 49.0 all-gather.5
  147.1 106.3 all-gather.7
  262.4 62.0 reduce-scatter.1
where the time goes:
time: 333 us
  waiting for transfers between devices  241 us (72%)
  blocking collectives  39.4 us (12%)
  other arithmetic  19.8 us (6%)
  matrix products  17.1 us (5%)
  between operations  15.1 us (5%)
    all_gather x1, waiting for transfers between devices, shards(): lax.all_gather(weight_new, 'grp', axis=1, tiled=True)  106 us
    reduce_scatter x1, waiting for transfers between devices, shards(): lax.psum_scatter(partial_sum.astype(jnp.bfloat16), 'tp', scatter_dimensio...  61.6 us
    all_gather x1, waiting for transfers between devices, shards(): cot_full = lax.all_gather(cotangent, 'tp', axis=0, tiled=True)  51.2 us
    psum x1, blocking collectives, shards(): total_sq = lax.psum(jnp.sum(grad * grad), ('grp', 'tp'))  39.4 us
    all_gather x1, waiting for transfers between devices, shards(): grad = add_terms(lax.all_gather(acts, 'grp', axis=0, tiled=True), cot_full)  20.3 us
    convert_element_type x1, other arithmetic, shards(): weight_new = (old - learn_rate * (m_hat / (jnp.sqrt(v_hat) + adam_eps) +...  18.3 us
    dot_general x1, matrix products, shards(): jnp.dot(roll_acts, lax.all_gather(weight_new, 'grp', axis=1, tiled=True),...  8.77 us
    dot_general x1, matrix products, add_terms(): lax.dot_general(left, right, (((0,), (0,)), ((), ())), preferred_element_...  8.31 us
  transfers between devices with their start and end apart: 4, of which 4 were waited for; matrix products, arithmetic and copies ran while one was open for 0% of the time, Pallas kernels for 0%

commit v1 on v0

--- a/solution.py
+++ b/solution.py
@@ -13,6 +13,18 @@
 step_count = 10
 
 
+def collect(x, axis, dim):
+    ways, here, turn = (lax.axis_size(axis), lax.axis_index(axis), x.shape[dim])
+    line, have = (x, 1)
+    while have < ways:
+        line = jnp.concatenate(
+            [line, lax.ppermute(line, axis, [(d, (d - have) % ways) for d in range(ways)])],
+            axis=dim,
+        )
+        have = 2 * have
+    return jnp.roll(line, here * turn, axis=dim)
+
+
 def add_terms(left, right):
     return lax.dot_general(
         left, right, (((0,), (0,)), ((), ())), preferred_element_type=jnp.float32
@@ -21,7 +33,7 @@
 
 def shards(acts, cotangent, weight, moment, second, roll_acts, live):
     cot_full = lax.all_gather(cotangent, "tp", axis=0, tiled=True)
-    grad = add_terms(lax.all_gather(acts, "grp", axis=0, tiled=True), cot_full)
+    grad = add_terms(collect(acts, "grp", 0), cot_full)
     total_sq = lax.psum(jnp.sum(grad * grad), ("grp", "tp"))
     factor = jnp.minimum(1.0, 1.0 / jnp.sqrt(total_sq / (E * D) + 1e-06))
     clipped = grad * factor

time: 333 us -> 314 us (0.943)
  waiting for transfers between devices: 241 us -> 217 us
    all_gather x1, waiting for transfers between devices: 51.2 us -> 30.6 us  [shards(): cot_full = lax.all_gather(cotangent, 'tp', axis=0, tiled=True)]
    all_gather x1 -> x0, waiting for transfers between devices: 20.3 us -> none  [shards(): grad = add_terms(lax.all_gather(acts, 'grp', axis=0, tiled=True), cot_full)]
    ppermute x0 -> x2, waiting for transfers between devices: none -> 17.2 us  [collect(): lax.ppermute(line, axis, [(d, (d - have) % ways) for d in range(ways)])]
  transfers between devices with their start and end apart: 4 -> 5, of which waited for: 4 -> 5; matrix products, arithmetic and copies ran while one was open for 0% -> 1% of each run, Pallas kernels for 0% -> 0%
where the time goes in v1:
time: 314 us
  waiting for transfers between devices  217 us (69%)
  blocking collectives  39.4 us (13%)
  other arithmetic  20.8 us (7%)
  matrix products  16.7 us (5%)
  between operations  15.1 us (5%)
  starting transfers between devices  3.21 us (1%)
    all_gather x1, waiting for transfers between devices, shards(): lax.all_gather(weight_new, 'grp', axis=1, tiled=True)  106 us
    reduce_scatter x1, waiting for transfers between devices, shards(): lax.psum_scatter(partial_sum.astype(jnp.bfloat16), 'tp', scatter_dimensio...  61.6 us
    psum x1, blocking collectives, shards(): total_sq = lax.psum(jnp.sum(grad * grad), ('grp', 'tp'))  39.4 us
    all_gather x1, waiting for transfers between devices, shards(): cot_full = lax.all_gather(cotangent, 'tp', axis=0, tiled=True)  30.6 us
    convert_element_type x1, other arithmetic, shards(): weight_new = (old - learn_rate * (m_hat / (jnp.sqrt(v_hat) + adam_eps) +...  18.3 us
    ppermute x2, waiting for transfers between devices, collect(): lax.ppermute(line, axis, [(d, (d - have) % ways) for d in range(ways)])  17.2 us
    dot_general x1, matrix products, shards(): jnp.dot(roll_acts, lax.all_gather(weight_new, 'grp', axis=1, tiled=True),...  8.77 us
    dot_general x1, matrix products, add_terms(): lax.dot_general(left, right, (((0,), (0,)), ((), ())), preferred_element_...  7.98 us
  transfers between devices with their start and end apart: 5, of which 5 were waited for; matrix products, arithmetic and copies ran while one was open for 1% of the time, Pallas kernels for 0%

profile of v1, /device:TPU:0, one launch (start us, length us, event | category | flops | bytes accessed | tf_op | source)
XLA Modules:
  0.0 313.9 jit_solution(9192174021277609644)
XLA Ops:
  7.2 0.0 copy-start
  7.2 0.0 all-gather.3.cloned.1.call-start
  7.2 0.7 all-gather.3.cloned.1.call-update
  7.9 0.0 all-gather.5.cloned.1.call-start
  8.0 2.5 collective-permute-start
  10.4 4.2 %collective-permute-done = bf16[128,1024]{1,0:T(8,128)(2,1)S(1)} collective-permute-done((bf16[128,1024]{1,0:T(8,128)(2,1)}, bf16[128,1024]{1,0:T(8,128)(2,1)S(1)}, u32[]{:S(2)}, u32[]{:S(2)}) %collective-permute-start) | collective-permute-done | bytes 262176 | tf_op jit(solution)/shard_map/ppermute | solution.py:21
  14.6 1.0 pad_maximum_fusion
  15.6 0.6 collective-permute-start.1
  16.2 1.0 constant_dynamic-update-slice_fusion.5
  17.2 13.0 %collective-permute-done.1 = bf16[256,1024]{1,0:T(8,128)(2,1)S(1)} collective-permute-done((bf16[256,1024]{1,0:T(8,128)(2,1)S(1)}, bf16[256,1024]{1,0:T(8,128)(2,1)S(1)}, u32[]{:S(2)}, u32[]{:S(2)}) %collective-permute-start.1) | collective-permute-done | bytes 524320 | tf_op jit(solution)/shard_map/ppermute | solution.py:21
  30.3 1.0 constant_dynamic-update-slice_fusion.2
  31.3 30.6 %all-gather.3.cloned.1.call-done = bf16[512,2048]{1,0:T(8,128)(2,1)} async-done(((bf16[64,2048]{1,0:T(8,128)(2,1)}), bf16[512,2048]{1,0:T(8,128)(2,1)}) %all-gather.3.cloned.1.call-update) | async-done | bytes 2097168 | tf_op jit(solution)/shard_map/all_gather | solution.py:35
  62.0 8.0 %multiply_reduce_fusion = (f32[]{:T(128)}, f32[1024,2048]{1,0:T(8,128)}) fusion(bf16[512,2048]{1,0:T(8,128)(2,1)} %all-gather.3.cloned.1.call-done, bf16[1024,1024]{1,0:T(8,128)(2,1)S(1)} %constant_dynamic-update-slice_fusion, s32[]{:T(128)S(6)} %select_n.18), kind=kOutput, calls=%fused_computation.10 | convolution fusion | flops 2151677952 | bytes 11534344 | tf_op jit(solution)/shard_map/dot_general | solution.py:29
  69.9 39.4 %psum.7 = f32[]{:T(128)} all-reduce(f32[]{:T(128)} %get-tuple-element.6), channel_id=1, replica_groups=mesh['grp'=4,'tp'=8] {'grp','tp'}, use_global_device_ids=true, to_apply=%region_1.2 | all-reduce | flops 1 | bytes 8 | tf_op jit(solution)/shard_map/psum | solution.py:37
  110.0 18.3 %fusion.3 = (bf16[1024,2048]{1,0:T(8,128)(2,1)}, f32[1024,2048]{1,0:T(8,128)}, f32[1024,2048]{1,0:T(8,128)}) fusion(bf16[1024,2048]{1,0:T(8,128)(2,1)} %param.9, f32[1024,2048]{1,0:T(8,128)} %get-tuple-element.7, f32[]{:T(128)S(6)} %min.3, f32[1024,2048]{1,0:T(8,128)} %param.11, f32[1024,2048]{1,0:T(8,128)} %param.10), kind=kLoop, calls=%fused_computation.7 | loop fusion | flops 37748736 | bytes 50331652 | tf_op jit(solution)/shard_map/convert_element_type | solution.py:47
  128.3 0.0 all-gather.5.cloned.1.call-update
  128.4 0.0 reduce-scatter.2.cloned.1.call-start
  128.4 106.5 %all-gather.5.cloned.1.call-done = bf16[1024,8192]{1,0:T(8,128)(2,1)} async-done(((bf16[1024,2048]{1,0:T(8,128)(2,1)}), bf16[1024,8192]{1,0:T(8,128)(2,1)}) %all-gather.5.cloned.1.call-update) | async-done | bytes 16777232 | tf_op jit(solution)/shard_map/all_gather | solution.py:51
  234.9 0.0 copy-done
  234.9 8.8 %fusion = bf16[16,8192]{1,0:T(8,128)(2,1)} fusion(bf16[16,1024]{1,0:T(8,128)(2,1)S(1)} %copy-done, bf16[1024,8192]{1,0:T(8,128)(2,1)} %all-gather.5.cloned.1.call-done), kind=kOutput, calls=%fused_computation.4 | convolution fusion | flops 268566528 | bytes 17072128 | tf_op jit(solution)/shard_map/dot_general | solution.py:49
  243.6 0.0 reduce-scatter.2.cloned.1.call-update
  244.3 61.6 %reduce-scatter.2.cloned.1.call-done = bf16[16,1024]{1,0:T(8,128)(2,1)} async-done(((bf16[16,8192]{1,0:T(8,128)(2,1)}), bf16[16,1024]{1,0:T(8,128)(2,1)}) %reduce-scatter.2.cloned.1.call-update) | async-done | bytes 32784 | tf_op jit(solution)/shard_map/reduce_scatter | solution.py:54
  305.9 1.4 select_convert_fusion
  (5 shorter events, 0.1 us)
Async XLA Ops:
  7.2 227.7 %copy-start = (bf16[16,1024]{1,0:T(8,128)(2,1)S(1)}, bf16[16,1024]{1,0:T(8,128)(2,1)}, u32[]{:S(2)}) copy-start(bf16[16,1024]{1,0:T(8,128)(2,1)} %param.12) | copy-start | bytes 98308
  7.2 54.8 %all-gather.3.cloned.1.call-start = ((), (), s32[]{:S(2)}) async-start(), calls=%async_computation.1 | async-start | bytes 2359296 | tf_op jit(solution)/shard_map/all_gather | solution.py:35
  7.9 227.0 %all-gather.5.cloned.1.call-start = ((), (), s32[]{:S(2)}) async-start(), calls=%async_computation.2 | async-start | bytes 20971520 | tf_op jit(solution)/shard_map/all_gather | solution.py:51
  8.0 6.7 %collective-permute-start = (bf16[128,1024]{1,0:T(8,128)(2,1)}, bf16[128,1024]{1,0:T(8,128)(2,1)S(1)}, u32[]{:S(2)}, u32[]{:S(2)}) collective-permute-start(bf16[128,1024]{1,0:T(8,128)(2,1)} %param.7), channel_id=1, source_target_pairs={{0,24},{8,0},{16,8},{24,16},{1,25},{9,1},{17,9},{25,17},{2,26},{10... | collective-permute-start | bytes 786440 | tf_op jit(solution)/shard_map/ppermute | solution.py:21
  15.6 14.6 %collective-permute-start.1 = (bf16[256,1024]{1,0:T(8,128)(2,1)S(1)}, bf16[256,1024]{1,0:T(8,128)(2,1)S(1)}, u32[]{:S(2)}, u32[]{:S(2)}) collective-permute-start(bf16[256,1024]{1,0:T(8,128)(2,1)S(1)} %pad_maximum_fusion), channel_id=1, source_target_pairs={{0,16},{8,24},{16,0},{24,8},{1,17},{9,25},{17,1},{25,9},{2,18},{10... | collective-permute-start | bytes 1572872 | tf_op jit(solution)/shard_map/ppermute | solution.py:21
  128.4 177.5 %reduce-scatter.2.cloned.1.call-start = ((), (), s32[]{:S(2)}) async-start(), calls=%async_computation.3 | async-start | bytes 294912 | tf_op jit(solution)/shard_map/reduce_scatter | solution.py:54
Sparse Core Ops, SparseCore 0:
  10.1 51.7 all-gather.2
  128.5 106.3 all-gather.4
  243.8 62.0 reduce-scatter.1
